TPU v7x, 256 devices: a whole 4x4x8 slice. The times are simulated.
256 devices in a mesh: dp: 16 (over z_hi, y, core), seq: 16 (over x, z_lo).
Axes of the slice: x: 4, y: 4, z: 8 (z_hi: 2, z_lo: 4; z = z_hi * 4 + z_lo), core: 2. Of those that a mesh axis runs over, the one named last changes fastest.
Arguments:
- inputs: bfloat16 [2, 65536, 2048], P(None, 'seq', 'dp'), may hold values from -6 to 6
- cotangent: bfloat16 [2, 65536, 2048], P(None, 'seq', 'dp'), may hold values from -6 to 6
- kernel: bfloat16 [65536, 2048], P('seq', 'dp'), may hold values from -6 to 6
- factor_one: bfloat16 [256, 256], replicated, may hold values from -0.375 to 0.375
- factor_two: bfloat16 [256, 256], replicated, may hold values from -0.375 to 0.375
Outputs:
- grad_inputs: bfloat16 [2, 65536, 2048], P(None, 'seq', 'dp')
- grad_kernel: bfloat16 [65536, 2048], P('seq', 'dp')
- grad_factor_one: float32 [256, 256], replicated
- grad_factor_two: float32 [256, 256], replicated
All inputs are finite; a program needn't handle non-finite values.
Results may differ from a plain program's by a relative error of at most 0.0085.
Values may be sent and summed in bfloat16 or wider, within the bound.
A program may use at most 128 MiB of HBM per device.

v0:
```python
import math

import jax
import jax.numpy as jnp
from jax import lax
from jax.sharding import PartitionSpec as P


def within_blocks(factor, values):
    return jnp.einsum("cb,nabh->nach", factor, values, preferred_element_type=jnp.float32)


def within_blocks_back(factor, values):
    return jnp.einsum("cb,nach->nabh", factor, values, preferred_element_type=jnp.float32)


def across_blocks(factor, values):
    return jnp.einsum("ea,nach->nech", factor, values, preferred_element_type=jnp.float32)


def across_blocks_back(factor, values):
    return jnp.einsum("ea,nech->nach", factor, values, preferred_element_type=jnp.float32)


def pair_product(left, right):
    return jnp.einsum("nech,nach->ea", left, right, preferred_element_type=jnp.float32)


def on_device(inputs, cotangent, kernel, factor_one, factor_two):
    batch_count = inputs.shape[0]
    row_count = inputs.shape[1]
    channels = inputs.shape[2]
    block_size = factor_one.shape[0]
    block_count = factor_two.shape[0]
    local_blocks = row_count // block_size
    inputs_cube = inputs.reshape(batch_count, local_blocks, block_size, channels)
    grads_cube = cotangent.reshape(batch_count, local_blocks, block_size, channels)
    kernel_cube = kernel.reshape(local_blocks, block_size, channels)
    within_mix = within_blocks(factor_one, inputs_cube).astype(jnp.bfloat16)
    within_spread = lax.all_to_all(within_mix, "seq", split_axis=2, concat_axis=1, tiled=True)
    spectrum = across_blocks(factor_two, within_spread).astype(jnp.bfloat16)
    grad_within = within_blocks(factor_one, grads_cube).astype(jnp.bfloat16)
    grad_spread = lax.all_to_all(grad_within, "seq", split_axis=2, concat_axis=1, tiled=True)
    grad_spectrum = across_blocks(factor_two, grad_spread).astype(jnp.bfloat16)
    spectrum_home, grad_spectrum_home = (
        lax.all_to_all(spectrum, "seq", split_axis=1, concat_axis=2, tiled=True),
        lax.all_to_all(grad_spectrum, "seq", split_axis=1, concat_axis=2, tiled=True),
    )
    kernel_wide = kernel_cube.astype(jnp.float32)[None]
    weighted_home = (kernel_wide * spectrum_home.astype(jnp.float32)).astype(jnp.bfloat16)
    grad_weighted_home = (kernel_wide * grad_spectrum_home.astype(jnp.float32)).astype(jnp.bfloat16)
    kernel_terms = jnp.sum(
        grad_spectrum_home.astype(jnp.float32) * spectrum_home.astype(jnp.float32), axis=0
    )
    weighted, grad_weighted = (
        lax.all_to_all(weighted_home, "seq", split_axis=2, concat_axis=1, tiled=True),
        lax.all_to_all(grad_weighted_home, "seq", split_axis=2, concat_axis=1, tiled=True),
    )
    returned_spread = across_blocks_back(factor_two, weighted).astype(jnp.bfloat16)
    grad_returned_spread = across_blocks_back(factor_two, grad_weighted).astype(jnp.bfloat16)
    second_terms = pair_product(weighted, grad_spread) + pair_product(grad_weighted, within_spread)
    returned, grad_returned = (
        lax.all_to_all(returned_spread, "seq", split_axis=1, concat_axis=2, tiled=True),
        lax.all_to_all(grad_returned_spread, "seq", split_axis=1, concat_axis=2, tiled=True),
    )
    grad_inputs = within_blocks_back(factor_one, grad_returned).astype(jnp.bfloat16)
    first_terms = jnp.einsum(
        "nach,nabh->cb", returned, grads_cube, preferred_element_type=jnp.float32
    )
    first_terms = first_terms + jnp.einsum(
        "nach,nabh->cb", grad_returned, inputs_cube, preferred_element_type=jnp.float32
    )
    first_total, second_total = lax.psum((first_terms, second_terms), ("dp", "seq"))
    kernel_half = kernel_terms.astype(jnp.bfloat16)
    grad_kernel = kernel_half.reshape(row_count, channels)
    full_width = channels * lax.axis_size("dp")
    scale_first = 1.0 / math.sqrt(batch_count * block_count * full_width)
    scale_second = 1.0 / math.sqrt(batch_count * block_size * full_width)
    return (
        grad_inputs.reshape(batch_count, row_count, channels),
        grad_kernel,
        first_total * scale_first,
        second_total * scale_second,
    )


def solution(mesh):
    return jax.shard_map(
        on_device,
        mesh=mesh,
        in_specs=(P(None, "seq", "dp"), P(None, "seq", "dp"), P("seq", "dp"), P(), P()),
        out_specs=(P(None, "seq", "dp"), P("seq", "dp"), P(), P()),
        check_vma=False,
    )
```

profile of v0, /device:TPU:2, one launch (start us, length us, event | category | flops | bytes accessed | tf_op | source)
XLA Modules:
  0.0 732.7 jit_solution(2225070951256302418)
XLA Ops:
  7.2 3.8 convert_bitcast_fusion.2
  11.0 4.6 copy.99
  15.6 9.0 %all-to-all-start.4 = ((bf16[2,16,256,128]{3,1,0,2:T(8,128)(2,1)}), bf16[2,16,256,128]{3,1,0,2:T(8,128)(2,1)}, u32[]{:S(2)}, u32[]{:S(2)}) async-start(bf16[2,16,256,128]{3,1,0,2:T(8,128)(2,1)} %copy.99), calls=%async_computation.4 | async-start | bytes 4194304 | tf_op jit(solution)/shard_map/all_to_all | solution.py:40
  24.6 2.1 convert_bitcast_fusion.6
  26.7 4.6 copy.82
  31.3 41.4 %all-to-all-done.4 = bf16[2,16,256,128]{3,1,0,2:T(8,128)(2,1)} async-done(((bf16[2,16,256,128]{3,1,0,2:T(8,128)(2,1)}), bf16[2,16,256,128]{3,1,0,2:T(8,128)(2,1)}, u32[]{:S(2)}, u32[]{:S(2)}) %all-to-all-start.4) | async-done | bytes 2097184 | tf_op jit(solution)/shard_map/all_to_all | solution.py:40
  72.6 6.7 all-to-all-start
  79.3 2.4 copy.101
  81.7 1.4 copy-done.3
  83.1 2.5 convert_bitcast_fusion.1
  85.6 4.5 copy.103
  90.1 36.7 %all-to-all-done = bf16[2,16,256,128]{3,1,0,2:T(8,128)(2,1)} async-done(((bf16[2,16,256,128]{3,1,0,2:T(8,128)(2,1)}), bf16[2,16,256,128]{3,1,0,2:T(8,128)(2,1)}, u32[]{:S(2)}, u32[]{:S(2)}) %all-to-all-start) | async-done | bytes 2097184 | tf_op jit(solution)/shard_map/all_to_all | solution.py:43
  126.8 6.8 all-to-all-start.5
  133.6 2.4 copy.84
  136.0 1.4 copy-done.5
  137.4 2.4 convert_bitcast_fusion.5
  139.9 4.5 copy.86
  144.4 36.7 %all-to-all-done.5 = bf16[2,256,16,128]{3,2,0,1:T(8,128)(2,1)} async-done(((bf16[2,256,16,128]{3,2,0,1:T(8,128)(2,1)}), bf16[2,256,16,128]{3,2,0,1:T(8,128)(2,1)}, u32[]{:S(2)}, u32[]{:S(2)}) %all-to-all-start.5) | async-done | bytes 2097184 | tf_op jit(solution)/shard_map/all_to_all | solution.py:46
  181.1 6.9 all-to-all-start.1
  188.0 2.8 convert.11
  190.7 1.9 copy_convert_fusion
  192.6 2.5 copy.108
  195.1 40.3 %all-to-all-done.1 = bf16[2,256,16,128]{3,2,0,1:T(8,128)(2,1)} async-done(((bf16[2,256,16,128]{3,2,0,1:T(8,128)(2,1)}), bf16[2,256,16,128]{3,2,0,1:T(8,128)(2,1)}, u32[]{:S(2)}, u32[]{:S(2)}) %all-to-all-start.1) | async-done | bytes 2097184 | tf_op jit(solution)/shard_map/all_to_all | solution.py:47
  235.5 1.9 copy_convert_fusion.1
  237.4 0.6 copy.88
  237.9 1.6 copy-done.1
  239.5 0.7 copy-done.2
  240.2 2.4 fusion
  242.6 2.7 copy.109
  245.3 6.8 all-to-all-start.6
  252.1 4.3 copy.89
  256.4 43.2 %all-to-all-done.6 = bf16[2,16,256,128]{3,1,0,2:T(8,128)(2,1)} async-done(((bf16[2,16,256,128]{3,1,0,2:T(8,128)(2,1)}), bf16[2,16,256,128]{3,1,0,2:T(8,128)(2,1)}, u32[]{:S(2)}, u32[]{:S(2)}) %all-to-all-start.6) | async-done | bytes 2097184 | tf_op jit(solution)/shard_map/all_to_all | solution.py:56
  299.6 6.8 all-to-all-start.2
  306.4 2.4 copy.111
  308.8 1.3 copy-done.7
  310.1 2.4 convert_bitcast_fusion
  312.6 4.6 copy.113
  317.1 36.8 %all-to-all-done.2 = bf16[2,16,256,128]{3,1,0,2:T(8,128)(2,1)} async-done(((bf16[2,16,256,128]{3,1,0,2:T(8,128)(2,1)}), bf16[2,16,256,128]{3,1,0,2:T(8,128)(2,1)}, u32[]{:S(2)}, u32[]{:S(2)}) %all-to-all-start.2) | async-done | bytes 2097184 | tf_op jit(solution)/shard_map/all_to_all | solution.py:57
  353.9 6.8 all-to-all-start.7
  360.8 2.4 copy.91
  363.2 1.3 copy-done.8
  364.5 2.4 convert_bitcast_fusion.4
  367.0 4.5 copy.93
  371.5 36.8 %all-to-all-done.7 = bf16[2,256,16,128]{3,2,0,1:T(8,128)(2,1)} async-done(((bf16[2,256,16,128]{3,2,0,1:T(8,128)(2,1)}), bf16[2,256,16,128]{3,2,0,1:T(8,128)(2,1)}, u32[]{:S(2)}, u32[]{:S(2)}) %all-to-all-start.7) | async-done | bytes 2097184 | tf_op jit(solution)/shard_map/all_to_all | solution.py:63
  408.3 6.8 all-to-all-start.3
  415.1 0.3 all-reduce.3.cloned.1.call-start
  415.4 2.8 multiply_reduce_fusion
  418.2 1.6 copy.138
  419.7 1.9 copy.106
  421.7 1.2 copy.107
  422.9 0.7 copy-done.6
  423.6 3.0 fusion.37
  426.6 1.9 fusion.47
  428.6 2.2 copy.115
  430.7 0.7 fusion.29
  431.5 31.1 %all-to-all-done.3 = bf16[2,256,16,128]{3,2,0,1:T(8,128)(2,1)} async-done(((bf16[2,256,16,128]{3,2,0,1:T(8,128)(2,1)}), bf16[2,256,16,128]{3,2,0,1:T(8,128)(2,1)}, u32[]{:S(2)}, u32[]{:S(2)}) %all-to-all-start.3) | async-done | bytes 2097184 | tf_op jit(solution)/shard_map/all_to_all | solution.py:64
  462.6 2.3 copy.95
  464.9 1.3 copy-done.10
  466.2 1.4 fusion.52
  467.7 0.0 all-reduce.3.cloned.1.call-update
  467.7 3.7 convert_bitcast_fusion.3
  471.4 3.9 copy.97
  475.4 248.7 %all-reduce.3.cloned.1.call-done = (f32[256,256]{1,0:T(8,128)}, f32[256,256]{1,0:T(8,128)}) async-done(((f32[256,256]{1,0:T(8,128)}, f32[256,256]{1,0:T(8,128)}), (f32[256,256]{1,0:T(8,128)}, f32[256,256]{1,0:T(8,128)})) %all-reduce.3.cloned.1.call-update) | async-done | bytes 524304 | tf_op jit(solution)/shard_map/psum | solution.py:73
  724.0 1.9 broadcast_multiply_fusion
  (20 shorter events, 0.0 us)
Async XLA Ops:
  7.2 17.4 %copy-start = (bf16[2,4096,128]{2,1,0:T(8,128)(2,1)S(1)}, bf16[2,4096,128]{2,1,0:T(8,128)(2,1)}, u32[]{:S(2)}) copy-start(bf16[2,4096,128]{2,1,0:T(8,128)(2,1)} %param.6) | copy-start | bytes 6291460
  15.6 9.0 %copy-start.13 = (bf16[256,256]{1,0:T(8,128)(2,1)S(1)}, bf16[256,256]{1,0:T(8,128)(2,1)}, u32[]{:S(2)}) copy-start(bf16[256,256]{1,0:T(8,128)(2,1)} %param.8) | copy-start | bytes 393220
  15.6 57.0 %all-to-all-start.4 = ((bf16[2,16,256,128]{3,1,0,2:T(8,128)(2,1)}), bf16[2,16,256,128]{3,1,0,2:T(8,128)(2,1)}, u32[]{:S(2)}, u32[]{:S(2)}) async-start(bf16[2,16,256,128]{3,1,0,2:T(8,128)(2,1)} %copy.99), calls=%async_computation.4 | async-start | bytes 4194304 | tf_op jit(solution)/shard_map/all_to_all | solution.py:40
  72.6 54.2 %all-to-all-start = ((bf16[2,16,256,128]{3,1,0,2:T(8,128)(2,1)}), bf16[2,16,256,128]{3,1,0,2:T(8,128)(2,1)}, u32[]{:S(2)}, u32[]{:S(2)}) async-start(bf16[2,16,256,128]{3,1,0,2:T(8,128)(2,1)} %copy.82), calls=%async_computation | async-start | bytes 4194304 | tf_op jit(solution)/shard_map/all_to_all | solution.py:43
  79.3 3.8 copy-start.11
  81.7 1.4 copy-start.3
  126.8 54.3 %all-to-all-start.5 = ((bf16[2,256,16,128]{3,2,0,1:T(8,128)(2,1)}), bf16[2,256,16,128]{3,2,0,1:T(8,128)(2,1)}, u32[]{:S(2)}, u32[]{:S(2)}) async-start(bf16[2,256,16,128]{3,2,0,1:T(8,128)(2,1)} %copy.103), calls=%async_computation.5 | async-start | bytes 4194304 | tf_op jit(solution)/shard_map/all_to_all | solution.py:46
  136.0 1.4 copy-start.5
  181.1 54.4 %all-to-all-start.1 = ((bf16[2,256,16,128]{3,2,0,1:T(8,128)(2,1)}), bf16[2,256,16,128]{3,2,0,1:T(8,128)(2,1)}, u32[]{:S(2)}, u32[]{:S(2)}) async-start(bf16[2,256,16,128]{3,2,0,1:T(8,128)(2,1)} %copy.86), calls=%async_computation.1 | async-start | bytes 4194304 | tf_op jit(solution)/shard_map/all_to_all | solution.py:47
  237.4 2.2 copy-start.1
  237.4 2.9 copy-start.2
  245.3 54.3 %all-to-all-start.6 = ((bf16[2,16,256,128]{3,1,0,2:T(8,128)(2,1)}), bf16[2,16,256,128]{3,1,0,2:T(8,128)(2,1)}, u32[]{:S(2)}, u32[]{:S(2)}) async-start(bf16[2,16,256,128]{3,1,0,2:T(8,128)(2,1)} %copy.109), calls=%async_computation.6 | async-start | bytes 4194304 | tf_op jit(solution)/shard_map/all_to_all | solution.py:56
  299.6 54.3 %all-to-all-start.2 = ((bf16[2,16,256,128]{3,1,0,2:T(8,128)(2,1)}), bf16[2,16,256,128]{3,1,0,2:T(8,128)(2,1)}, u32[]{:S(2)}, u32[]{:S(2)}) async-start(bf16[2,16,256,128]{3,1,0,2:T(8,128)(2,1)} %copy.89), calls=%async_computation.2 | async-start | bytes 4194304 | tf_op jit(solution)/shard_map/all_to_all | solution.py:57
  308.8 1.3 copy-start.7
  353.9 54.3 %all-to-all-start.7 = ((bf16[2,256,16,128]{3,2,0,1:T(8,128)(2,1)}), bf16[2,256,16,128]{3,2,0,1:T(8,128)(2,1)}, u32[]{:S(2)}, u32[]{:S(2)}) async-start(bf16[2,256,16,128]{3,2,0,1:T(8,128)(2,1)} %copy.113), calls=%async_computation.7 | async-start | bytes 4194304 | tf_op jit(solution)/shard_map/all_to_all | solution.py:63
  363.2 1.3 copy-start.8
  408.3 54.3 %all-to-all-start.3 = ((bf16[2,256,16,128]{3,2,0,1:T(8,128)(2,1)}), bf16[2,256,16,128]{3,2,0,1:T(8,128)(2,1)}, u32[]{:S(2)}, u32[]{:S(2)}) async-start(bf16[2,256,16,128]{3,2,0,1:T(8,128)(2,1)} %copy.93), calls=%async_computation.3 | async-start | bytes 4194304 | tf_op jit(solution)/shard_map/all_to_all | solution.py:64
  415.1 308.9 %all-reduce.3.cloned.1.call-start = ((), (), s32[]{:S(2)}) async-start(), calls=%async_computation.8 | async-start | bytes 1048576 | tf_op jit(solution)/shard_map/psum | solution.py:73
  421.7 2.0 copy-start.6
  423.6 3.0 copy-start.4
  423.6 3.0 copy-start.9
  462.6 3.7 copy-start.12
  464.9 1.3 copy-start.10
Sparse Core Ops, SparseCore 0:
  467.8 256.1 all-reduce.2
where the time goes:
time: 734 us; the launch traced here: 733 us
  waiting for transfers between devices  552 us (75%)
  local copies, waits for them, and re-layouts  69.9 us (10%)
  starting transfers between devices  57 us (8%)
  matrix products  26.5 us (4%)
  between operations  14.2 us (2%)
  other arithmetic  13.5 us (2%)
    psum x1, waiting for transfers between devices, on_device(): lax.psum((first_terms, second_terms), ('dp', 'seq'))  249 us
    all_to_all x1, waiting for transfers between devices, on_device(): lax.all_to_all(weighted_home, 'seq', split_axis=2, concat_axis=1, tiled=T...  43.2 us
    all_to_all x1, waiting for transfers between devices, on_device(): lax.all_to_all(within_mix, 'seq', split_axis=2, concat_axis=1, tiled=True)  41.4 us
    all_to_all x1, waiting for transfers between devices, on_device(): lax.all_to_all(grad_spectrum, 'seq', split_axis=1, concat_axis=2, tiled=T...  40.3 us
    all_to_all x1, waiting for transfers between devices, on_device(): lax.all_to_all(grad_weighted_home, 'seq', split_axis=2, concat_axis=1, ti...  36.8 us
    all_to_all x1, waiting for transfers between devices, on_device(): lax.all_to_all(returned_spread, 'seq', split_axis=1, concat_axis=2, tiled...  36.8 us
    all_to_all x1, waiting for transfers between devices, on_device(): lax.all_to_all(spectrum, 'seq', split_axis=1, concat_axis=2, tiled=True)  36.7 us
    all_to_all x1, waiting for transfers between devices, on_device(): lax.all_to_all(grad_within, 'seq', split_axis=2, concat_axis=1, tiled=True)  36.7 us
  transfers between devices with their start and end apart: 9, of which 9 were waited for; matrix products, arithmetic and copies ran while one was open for 11% of the time, Pallas kernels for 0%

commit v1 on v0

v1 whole, which is shorter than its diff:
```python
import functools
import math

import jax
import jax.numpy as jnp
from jax import lax
from jax.experimental import pallas as pl
from jax.experimental.pallas import tpu as pltpu
from jax.sharding import PartitionSpec as P

BF16 = jnp.bfloat16
F32 = jnp.float32
NN = (((1,), (0,)), ((), ()))
NT = (((1,), (1,)), ((), ()))
TN = (((0,), (0,)), ((), ()))


def dot(left, right, dims=NN):
    return lax.dot_general(left, right, dims, preferred_element_type=F32)


def put(ref, rows, value):
    ref[0, rows, :] = value[:, 0:128]
    ref[1, rows, :] = value[:, 128:256]


def take(ref, rows):
    return jnp.concatenate([ref[0, rows, :], ref[1, rows, :]], axis=1)


def kernel(
    seq_n, scale_one, scale_two,
    x_hbm, y_hbm, k_hbm, f1_ref, f2_ref,
    gi_hbm, gk_hbm, g1_out, g2_out,
    stage, send, recv, out_send, out_recv, out_stage,
    a_buf, g_buf, k_buf, gk_buf, c_buf, v_buf, f2t_ref,
    gf, red1, acc1, red2, acc2, zbuf, tot, red3, red4,
    load_sem, send_sem, recv_sem, osend_sem, orecv_sem, gsend_sem, grecv_sem, store_sem,
):
    me = lax.axis_index("seq")
    dp = lax.axis_index("dp")
    yc_n = 8
    zh = dp // yc_n
    yc = dp % yc_n
    other_dp = (1 - zh) * yc_n + yc

    def seq_peer(step):
        return lax.rem(me + step, seq_n)

    def yc_peer(step):
        return lax.rem(yc + step, yc_n)

    sources = (x_hbm.at[0], y_hbm.at[0], k_hbm, x_hbm.at[1], y_hbm.at[1])
    loads = []
    for at, source in enumerate(sources):
        loads.append(pltpu.make_async_copy(source, stage.at[at], load_sem.at[at]))
        loads[at].start()

    barrier = pltpu.get_barrier_semaphore()

    @pl.loop(1, seq_n)
    def _(step):
        pl.semaphore_signal(barrier, inc=1, device_id={"seq": seq_peer(step)}, device_id_type=pl.DeviceIdType.MESH)

    @pl.loop(1, yc_n)
    def _(step):
        pl.semaphore_signal(barrier, inc=1, device_id={"dp": zh * yc_n + yc_peer(step)}, device_id_type=pl.DeviceIdType.MESH)

    pl.semaphore_signal(barrier, inc=1, device_id={"dp": other_dp}, device_id_type=pl.DeviceIdType.MESH)

    eye_h = (lax.broadcasted_iota(jnp.int32, (128, 128), 0) == lax.broadcasted_iota(jnp.int32, (128, 128), 1)).astype(F32).astype(BF16)
    eye_b = (lax.broadcasted_iota(jnp.int32, (256, 256), 0) == lax.broadcasted_iota(jnp.int32, (256, 256), 1)).astype(F32).astype(BF16)

    def pack(at):
        @pl.loop(0, 8)
        def _(pair):
            base = pl.multiple_of(pair * 512, 512)
            first = dot(eye_h, stage[at, pl.ds(base, 256), :], NT)
            second = dot(eye_h, stage[at, pl.ds(base + 256, 256), :], NT)
            row = pl.multiple_of(pair * 16, 16)
            for group in range(16):
                both = jnp.concatenate([first[group * 8:group * 8 + 8], second[group * 8:group * 8 + 8]], axis=0)
                send[at, group, pl.ds(row, 16), :] = both.astype(BF16)

    def spread(source, target, send_at, recv_at):
        @pl.loop(1, seq_n)
        def _(step):
            peer = seq_peer(step)
            pltpu.make_async_remote_copy(
                src_ref=source.at[peer], dst_ref=target.at[me], send_sem=send_at, recv_sem=recv_at,
                device_id={"seq": peer}, device_id_type=pl.DeviceIdType.MESH,
            ).start()
        pltpu.make_async_copy(source.at[me], target.at[me], recv_at).start()

    def arrived(target, recv_at):
        pltpu.make_async_copy(target, target, recv_at).wait()

    def drained(source, target, send_at):
        part = source.at[pl.ds(0, source.shape[0] - 1)]
        pltpu.make_async_copy(part, target.at[pl.ds(0, source.shape[0] - 1)], send_at).wait()

    f2t_ref[...] = f2_ref[...].astype(F32).T.astype(BF16)
    gf[...] = jnp.zeros_like(gf)
    for at in range(5):
        loads[at].wait()
        pack(at)
        if at == 0:
            pl.semaphore_wait(barrier, seq_n - 1 + yc_n - 1 + 1)
        spread(send.at[at], recv.at[at], send_sem.at[at], recv_sem.at[at])

    def rows_of(ref, at, block):
        return ref[at, pl.ds(block * 2, 2)].reshape(256, 256)

    def compute(batch, x_at, y_at):
        @pl.loop(0, 8)
        def _(block):
            rows = pl.ds(pl.multiple_of(block * 256, 256), 256)
            put(a_buf, rows, dot(rows_of(recv, x_at, block), f1_ref[...], NT))
            put(g_buf, rows, dot(rows_of(recv, y_at, block), f1_ref[...], NT))
            if batch == 0:
                put(k_buf, rows, rows_of(recv, 2, block).astype(F32))

        @pl.loop(0, 8)
        def _(lane):
            rows = pl.ds(lane, 256, stride=8)
            a = take(a_buf, rows).astype(BF16)
            g = take(g_buf, rows).astype(BF16)
            k = take(k_buf, rows)
            s = dot(f2_ref[...], a).astype(BF16).astype(F32)
            h = dot(f2_ref[...], g).astype(BF16).astype(F32)
            z = (k * s).astype(BF16)
            w = (k * h).astype(BF16)
            if batch == 0:
                put(gk_buf, rows, h * s)
            else:
                put(gk_buf, rows, take(gk_buf, rows) + h * s)
            put(c_buf, rows, dot(f2t_ref[...], z))
            put(v_buf, rows, dot(f2t_ref[...], w))
            gf[256:512, :] += dot(z, g, NT) + dot(w, a, NT)

        @pl.loop(0, 8)
        def _(block):
            rows = pl.ds(pl.multiple_of(block * 256, 256), 256)
            c = take(c_buf, rows).astype(BF16)
            v = take(v_buf, rows).astype(BF16)
            out_send[batch, pl.ds(block * 2, 2)] = dot(v, f1_ref[...]).astype(BF16).reshape(2, 128, 256)
            gf[0:256, :] += dot(c, rows_of(recv, y_at, block), TN) + dot(v, rows_of(recv, x_at, block), TN)
            if batch == 1:
                out_send[2, pl.ds(block * 2, 2)] = take(gk_buf, rows).astype(BF16).reshape(2, 128, 256)

    for at in (0, 1, 2):
        arrived(recv.at[at], recv_sem.at[at])
    compute(0, 0, 1)
    spread(out_send.at[0], out_recv.at[0], osend_sem.at[0], orecv_sem.at[0])
    for at in (3, 4):
        arrived(recv.at[at], recv_sem.at[at])
    compute(1, 3, 4)

    @pl.loop(1, yc_n)
    def _(step):
        peer = yc_peer(step)
        pltpu.make_async_remote_copy(
            src_ref=gf.at[pl.ds(pl.multiple_of(peer * 64, 64), 64)], dst_ref=red1.at[yc],
            send_sem=gsend_sem.at[0], recv_sem=grecv_sem.at[0],
            device_id={"dp": zh * yc_n + peer}, device_id_type=pl.DeviceIdType.MESH,
        ).start()
    pltpu.make_async_copy(gf.at[pl.ds(pl.multiple_of(yc * 64, 64), 64)], red1.at[yc], grecv_sem.at[0]).start()
    arrived(red1, grecv_sem.at[0])
    for block in range(8):
        rows = slice(block * 8, block * 8 + 8)
        total = red1[0, rows, :]
        for slot in range(1, yc_n):
            total = total + red1[slot, rows, :]
        acc1[block * 2] = total[:, 0:128]
        acc1[block * 2 + 1] = total[:, 128:256]
    spread(acc1, red2, gsend_sem.at[1], grecv_sem.at[1])
    spread(out_send.at[2], out_recv.at[2], osend_sem.at[2], orecv_sem.at[2])
    spread(out_send.at[1], out_recv.at[1], osend_sem.at[1], orecv_sem.at[1])

    stores = []

    def unpack(at, target):
        @pl.loop(0, 8)
        def _(pair):
            row = pl.multiple_of(pair * 16, 16)
            firsts, seconds = [], []
            for group in range(16):
                both = out_recv[at, group, pl.ds(row, 16), :].astype(F32)
                firsts.append(both[0:8])
                seconds.append(both[8:16])
            base = pl.multiple_of(pair * 512, 512)
            out_stage[at, pl.ds(base, 256), :] = dot(eye_b, jnp.concatenate(firsts, axis=0).astype(BF16), NT).astype(BF16)
            out_stage[at, pl.ds(base + 256, 256), :] = dot(eye_b, jnp.concatenate(seconds, axis=0).astype(BF16), NT).astype(BF16)
        copy = pltpu.make_async_copy(out_stage.at[at], target, store_sem.at[at])
        copy.start()
        stores.append(copy)

    arrived(out_recv.at[0], orecv_sem.at[0])
    unpack(0, gi_hbm.at[0])

    arrived(red2, grecv_sem.at[1])
    total = red2[0]
    for slot in range(1, 16):
        total = total + red2[slot]
    acc2[...] = total
    across = pltpu.make_async_remote_copy(
        src_ref=acc2, dst_ref=zbuf, send_sem=gsend_sem.at[2], recv_sem=grecv_sem.at[2],
        device_id={"dp": other_dp}, device_id_type=pl.DeviceIdType.MESH,
    )
    across.start()
    across.wait()
    tot[...] = acc2[...] + zbuf[...]

    @pl.loop(1, seq_n)
    def _(step):
        pltpu.make_async_remote_copy(
            src_ref=tot, dst_ref=red3.at[me], send_sem=gsend_sem.at[3], recv_sem=grecv_sem.at[3],
            device_id={"seq": seq_peer(step)}, device_id_type=pl.DeviceIdType.MESH,
        ).start()
    pltpu.make_async_copy(tot, red3.at[me], grecv_sem.at[3]).start()
    arrived(red3, grecv_sem.at[3])

    @pl.loop(1, yc_n)
    def _(step):
        pltpu.make_async_remote_copy(
            src_ref=red3, dst_ref=red4.at[yc], send_sem=gsend_sem.at[4], recv_sem=grecv_sem.at[4],
            device_id={"dp": zh * yc_n + yc_peer(step)}, device_id_type=pl.DeviceIdType.MESH,
        ).start()
    pltpu.make_async_copy(red3, red4.at[yc], grecv_sem.at[4]).start()

    arrived(out_recv.at[2], orecv_sem.at[2])
    unpack(2, gk_hbm)
    arrived(red4, grecv_sem.at[4])
    for slot in range(yc_n):
        for block in range(8):
            out, scale = (g1_out, scale_one) if slot < 4 else (g2_out, scale_two)
            rows = slice((slot % 4) * 64 + block * 8, (slot % 4) * 64 + block * 8 + 8)
            out[rows, 0:128] = red4[slot, block * 2] * scale
            out[rows, 128:256] = red4[slot, block * 2 + 1] * scale
    arrived(out_recv.at[1], orecv_sem.at[1])
    unpack(1, gi_hbm.at[1])

    for at in range(5):
        drained(send.at[at], recv.at[at], send_sem.at[at])
    for at in range(3):
        drained(out_send.at[at], out_recv.at[at], osend_sem.at[at])
    drained(red1, red1, gsend_sem.at[0])
    drained(red2, red2, gsend_sem.at[1])
    drained(red3, red3, gsend_sem.at[3])
    drained(red4, red4, gsend_sem.at[4])
    for copy in stores:
        copy.wait()


def on_device(mesh, inputs, cotangent, kernel_rows, factor_one, factor_two):
    seq_n = mesh.shape["seq"]
    width = mesh.shape["dp"] * inputs.shape[2]
    batch = inputs.shape[0]
    scale_one = 1.0 / math.sqrt(batch * factor_two.shape[0] * width)
    scale_two = 1.0 / math.sqrt(batch * factor_one.shape[0] * width)
    anywhere = pl.BlockSpec(memory_space=pl.ANY)
    vmem = pl.BlockSpec(memory_space=pltpu.VMEM)
    square = pltpu.VMEM((2, 2048, 128), F32)
    return pl.pallas_call(
        functools.partial(kernel, seq_n, scale_one, scale_two),
        out_shape=(
            jax.ShapeDtypeStruct(inputs.shape, BF16),
            jax.ShapeDtypeStruct(kernel_rows.shape, BF16),
            jax.ShapeDtypeStruct((256, 256), F32),
            jax.ShapeDtypeStruct((256, 256), F32),
        ),
        in_specs=[anywhere, anywhere, anywhere, vmem, vmem],
        out_specs=(anywhere, anywhere, vmem, vmem),
        scratch_shapes=[
            pltpu.VMEM((5, 4096, 128), BF16),
            pltpu.VMEM((5, 16, 128, 256), BF16),
            pltpu.VMEM((5, 16, 128, 256), BF16),
            pltpu.VMEM((3, 16, 128, 256), BF16),
            pltpu.VMEM((3, 16, 128, 256), BF16),
            pltpu.VMEM((3, 4096, 128), BF16),
            square, square, square, square, square, square,
            pltpu.VMEM((256, 256), BF16),
            pltpu.VMEM((512, 256), F32),
            pltpu.VMEM((8, 64, 256), F32),
            pltpu.VMEM((16, 8, 128), F32),
            pltpu.VMEM((16, 8, 128), F32),
            pltpu.VMEM((8, 128), F32),
            pltpu.VMEM((8, 128), F32),
            pltpu.VMEM((8, 128), F32),
            pltpu.VMEM((16, 8, 128), F32),
            pltpu.VMEM((8, 16, 8, 128), F32),
            pltpu.SemaphoreType.DMA((5,)),
            pltpu.SemaphoreType.DMA((5,)),
            pltpu.SemaphoreType.DMA((5,)),
            pltpu.SemaphoreType.DMA((3,)),
            pltpu.SemaphoreType.DMA((3,)),
            pltpu.SemaphoreType.DMA((5,)),
            pltpu.SemaphoreType.DMA((5,)),
            pltpu.SemaphoreType.DMA((3,)),
        ],
        compiler_params=pltpu.CompilerParams(
            collective_id=0, has_side_effects=True, vmem_limit_bytes=60 * 1024 * 1024
        ),
    )(inputs, cotangent, kernel_rows, factor_one, factor_two)


def solution(mesh):
    return jax.shard_map(
        functools.partial(on_device, mesh),
        mesh=mesh,
        in_specs=(P(None, "seq", "dp"), P(None, "seq", "dp"), P("seq", "dp"), P(), P()),
        out_specs=(P(None, "seq", "dp"), P("seq", "dp"), P(), P()),
        check_vma=False,
    )
```

time: 734 us -> 222 us (0.30)
  waiting for transfers between devices: 552 us -> 0 us
  Pallas kernels: 0 us -> 213 us
  local copies, waits for them, and re-layouts: 69.9 us -> 5.53 us
  starting transfers between devices: 57 us -> 0 us
  matrix products: 26.5 us -> 0 us
  between operations: 14.2 us -> 0.66 us
  other arithmetic: 13.5 us -> 0 us
    all_to_all x8 -> x0, waiting for transfers between devices: 303 us -> none  [the longest x1 43.2 us: on_device(): lax.all_to_all(weighted_home, 'seq', split_axis=2, concat_axis=1, tiled=T...]
    psum x1 -> x0, waiting for transfers between devices: 249 us -> none  [on_device(): lax.psum((first_terms, second_terms), ('dp', 'seq'))]
    pallas_call x0 -> x1, Pallas kernels: none -> 213 us  [on_device(): pl.pallas_call(functools.partial(kernel, seq_n, scale_one, scale_two), ou...]
    all_to_all x8 -> x0, starting transfers between devices: 56.7 us -> none  [the longest x1 9.04 us: on_device(): lax.all_to_all(within_mix, 'seq', split_axis=2, concat_axis=1, tiled=True)]
    convert_element_type x12 -> x0, local copies, waits for them, and re-layouts: 42.5 us -> none  [the longest x1 4.57 us: on_device(): within_mix = within_blocks(factor_one, inputs_cube).astype(jnp.bfloat16)]
    dot_general x11 -> x0, matrix products: 26.5 us -> none  [the longest x2 5.9 us: within_blocks(): jnp.einsum('cb,nabh->nach', factor, values, preferred_element_type=jnp.fl...]
    all_to_all x6 -> x0, local copies, waits for them, and re-layouts: 14.1 us -> none  [the longest x1 2.44 us: on_device(): lax.all_to_all(within_mix, 'seq', split_axis=2, concat_axis=1, tiled=True)]
    convert_element_type x4 -> x0, other arithmetic: 8.85 us -> none  [the longest x1 2.76 us: on_device(): kernel_wide = kernel_cube.astype(jnp.float32)[None]]
  transfers between devices with their start and end apart: 9 -> 0, of which waited for: 9 -> 0; matrix products, arithmetic and copies ran while one was open for 11% -> 0% of each run, Pallas kernels for 0% -> 0%
where the time goes in v1:
time: 222 us; the launch traced here: 220 us
  Pallas kernels  213 us (96%)
  local copies, waits for them, and re-layouts  5.53 us (2%)
    pallas_call x1, Pallas kernels, on_device(): pl.pallas_call(functools.partial(kernel, seq_n, scale_one, scale_two), ou...  213 us
    unnamed x10, local copies, waits for them, and re-layouts  5.53 us

profile of v1, /device:TPU:2, one launch (start us, length us, event | category | flops | bytes accessed | tf_op | source)
XLA Modules:
  0.0 219.5 jit_solution(5028122189413105446)
XLA Ops:
  0.6 213.3 %shard_map.84 = (bf16[2,4096,128]{2,1,0:T(8,128)(2,1)}, bf16[4096,128]{1,0:T(8,128)(2,1)}, f32[256,256]{1,0:T(8,128)}, f32[256,256]{1,0:T(8,128)}) custom-call(bf16[2,4096,128]{2,1,0:T(8,128)(2,1)} %x_hbm.1, bf16[2,4096,128]{2,1,0:T(8,128)(2,1)} %y_hbm.1, bf16[4096,128]{1,0:T(8,128)(2,1)} %k_hbm.1, bf16[256,256]{1,0:T(8,128)(2,1)} %f1_ref.1, ...), custom_call_target="tpu_custom_call" | custom-call | tf_op jit(solution)/shard_map/pallas_call | solution.py:264
  213.9 0.0 copy-start
  214.0 0.0 copy-start.2
  214.0 3.1 %copy.13 = bf16[2,4096,128]{2,1,0:T(8,128)(2,1)} copy(bf16[2,4096,128]{2,1,0:T(8,128)(2,1)} %get-tuple-element.8) | data formatting | bytes 4194304
  217.1 0.0 copy-done
  217.1 0.0 copy-start.1
  217.1 1.0 copy.14
  218.1 0.0 copy-done.2
  218.1 0.7 copy.15
  218.8 0.0 copy-done.1
  218.8 0.7 copy.16
Async XLA Ops:
  213.9 3.2 %copy-start = (bf16[4096,128]{1,0:T(8,128)(2,1)S(1)}, bf16[4096,128]{1,0:T(8,128)(2,1)}, u32[]{:S(2)}) copy-start(bf16[4096,128]{1,0:T(8,128)(2,1)} %get-tuple-element.9) | copy-start | bytes 3145732
  214.0 4.1 %copy-start.2 = (f32[256,256]{1,0:T(8,128)S(1)}, f32[256,256]{1,0:T(8,128)}, u32[]{:S(2)}) copy-start(f32[256,256]{1,0:T(8,128)} %get-tuple-element.10) | copy-start | bytes 786436
  217.1 1.7 copy-start.1

commit v2 on v1

--- a/solution.py
+++ b/solution.py
@@ -30,12 +30,12 @@
 
 def kernel(
     seq_n, scale_one, scale_two,
-    x_hbm, y_hbm, k_hbm, f1_ref, f2_ref,
+    x_hbm, y_hbm, k_hbm, f1_hbm, f2_hbm,
     gi_hbm, gk_hbm, g1_out, g2_out,
-    stage, send, recv, out_send, out_recv, out_stage,
-    a_buf, g_buf, k_buf, gk_buf, c_buf, v_buf, f2t_ref,
+    stage, send, recv, out_send, out_recv,
+    a_buf, g_buf, k_buf, gk_buf, c_buf, v_buf, f1_ref, f2_ref, f2t_ref,
     gf, red1, acc1, red2, acc2, zbuf, tot, red3, red4,
-    load_sem, send_sem, recv_sem, osend_sem, orecv_sem, gsend_sem, grecv_sem, store_sem,
+    first_sem, load_sem, send_sem, recv_sem, osend_sem, orecv_sem, gsend_sem, grecv_sem, entered,
 ):
     me = lax.axis_index("seq")
     dp = lax.axis_index("dp")
@@ -51,10 +51,19 @@
         return lax.rem(yc + step, yc_n)
 
     sources = (x_hbm.at[0], y_hbm.at[0], k_hbm, x_hbm.at[1], y_hbm.at[1])
-    loads = []
-    for at, source in enumerate(sources):
-        loads.append(pltpu.make_async_copy(source, stage.at[at], load_sem.at[at]))
-        loads[at].start()
+    first_loads = []
+    for quarter in range(4):
+        rows = pl.ds(quarter * 1024, 1024)
+        first_loads.append(pltpu.make_async_copy(sources[0].at[rows], stage.at[0, rows], first_sem.at[quarter]))
+    loads = [None]
+    for at in range(1, 5):
+        loads.append(pltpu.make_async_copy(sources[at], stage.at[at], load_sem.at[at]))
+    factor_loads = (
+        pltpu.make_async_copy(f1_hbm, f1_ref, load_sem.at[0]),
+        pltpu.make_async_copy(f2_hbm, f2_ref, load_sem.at[5]),
+    )
+    for copy in (*first_loads, *loads[1:], *factor_loads):
+        copy.start()
 
     barrier = pltpu.get_barrier_semaphore()
 
@@ -66,13 +75,15 @@
     def _(step):
         pl.semaphore_signal(barrier, inc=1, device_id={"dp": zh * yc_n + yc_peer(step)}, device_id_type=pl.DeviceIdType.MESH)
 
-    pl.semaphore_signal(barrier, inc=1, device_id={"dp": other_dp}, device_id_type=pl.DeviceIdType.MESH)
+    @pl.when(zh == 0)
+    def _():
+        pl.semaphore_signal(barrier, inc=1, device_id={"dp": other_dp}, device_id_type=pl.DeviceIdType.MESH)
 
     eye_h = (lax.broadcasted_iota(jnp.int32, (128, 128), 0) == lax.broadcasted_iota(jnp.int32, (128, 128), 1)).astype(F32).astype(BF16)
     eye_b = (lax.broadcasted_iota(jnp.int32, (256, 256), 0) == lax.broadcasted_iota(jnp.int32, (256, 256), 1)).astype(F32).astype(BF16)
 
-    def pack(at):
-        @pl.loop(0, 8)
+    def pack(at, low, high):
+        @pl.loop(low, high)
         def _(pair):
             base = pl.multiple_of(pair * 512, 512)
             first = dot(eye_h, stage[at, pl.ds(base, 256), :], NT)
@@ -92,6 +103,29 @@
             ).start()
         pltpu.make_async_copy(source.at[me], target.at[me], recv_at).start()
 
+    def spread_quarter(at, quarter):
+        rows = pl.ds(quarter * 32, 32)
+
+        @pl.loop(1, seq_n)
+        def _(step):
+            peer = seq_peer(step)
+            pltpu.make_async_remote_copy(
+                src_ref=out_send.at[at, peer, rows], dst_ref=out_recv.at[at, me, rows],
+                send_sem=osend_sem.at[at, quarter], recv_sem=orecv_sem.at[at, quarter],
+                device_id={"seq": peer}, device_id_type=pl.DeviceIdType.MESH,
+            ).start()
+        pltpu.make_async_copy(out_send.at[at, me, rows], out_recv.at[at, me, rows], orecv_sem.at[at, quarter]).start()
+
+    def quarter_arrived(at, quarter):
+        whole = out_recv.at[at, :, pl.ds(quarter * 32, 32)]
+        pltpu.make_async_copy(whole, whole, orecv_sem.at[at, quarter]).wait()
+
+    def quarter_drained(at, quarter):
+        rows = pl.ds(quarter * 32, 32)
+        pltpu.make_async_copy(
+            out_send.at[at, pl.ds(0, seq_n - 1), rows], out_recv.at[at, pl.ds(0, seq_n - 1), rows], osend_sem.at[at, quarter]
+        ).wait()
+
     def arrived(target, recv_at):
         pltpu.make_async_copy(target, target, recv_at).wait()
 
@@ -99,14 +133,34 @@
         part = source.at[pl.ds(0, source.shape[0] - 1)]
         pltpu.make_async_copy(part, target.at[pl.ds(0, source.shape[0] - 1)], send_at).wait()
 
+    for quarter in range(4):
+        first_loads[quarter].wait()
+        pack(0, quarter * 2, quarter * 2 + 2)
+        if quarter == 0:
+            pl.semaphore_wait(barrier, seq_n - 1 + yc_n - 1 + zh)
+        rows = pl.ds(quarter * 32, 32)
+
+        @pl.loop(1, seq_n)
+        def _(step):
+            peer = seq_peer(step)
+            pltpu.make_async_remote_copy(
+                src_ref=send.at[0, peer, rows], dst_ref=recv.at[0, me, rows], send_sem=send_sem.at[0], recv_sem=recv_sem.at[0],
+                device_id={"seq": peer}, device_id_type=pl.DeviceIdType.MESH,
+            ).start()
+        pltpu.make_async_copy(send.at[0, me, rows], recv.at[0, me, rows], recv_sem.at[0]).start()
+
+    @pl.when(zh == 1)
+    def _():
+        pl.semaphore_signal(entered, inc=1, device_id={"dp": other_dp}, device_id_type=pl.DeviceIdType.MESH)
+
+    for at in range(1, 5):
+        loads[at].wait()
+        pack(at, 0, 8)
+        spread(send.at[at], recv.at[at], send_sem.at[at], recv_sem.at[at])
+    for copy in factor_loads:
+        copy.wait()
     f2t_ref[...] = f2_ref[...].astype(F32).T.astype(BF16)
     gf[...] = jnp.zeros_like(gf)
-    for at in range(5):
-        loads[at].wait()
-        pack(at)
-        if at == 0:
-            pl.semaphore_wait(barrier, seq_n - 1 + yc_n - 1 + 1)
-        spread(send.at[at], recv.at[at], send_sem.at[at], recv_sem.at[at])
 
     def rows_of(ref, at, block):
         return ref[at, pl.ds(block * 2, 2)].reshape(256, 256)
@@ -151,7 +205,8 @@
     for at in (0, 1, 2):
         arrived(recv.at[at], recv_sem.at[at])
     compute(0, 0, 1)
-    spread(out_send.at[0], out_recv.at[0], osend_sem.at[0], orecv_sem.at[0])
+    for quarter in range(4):
+        spread_quarter(0, quarter)
     for at in (3, 4):
         arrived(recv.at[at], recv_sem.at[at])
     compute(1, 3, 4)
@@ -165,6 +220,8 @@
             device_id={"dp": zh * yc_n + peer}, device_id_type=pl.DeviceIdType.MESH,
         ).start()
     pltpu.make_async_copy(gf.at[pl.ds(pl.multiple_of(yc * 64, 64), 64)], red1.at[yc], grecv_sem.at[0]).start()
+    spread_quarter(2, 0)
+    spread_quarter(2, 1)
     arrived(red1, grecv_sem.at[0])
     for block in range(8):
         rows = slice(block * 8, block * 8 + 8)
@@ -174,13 +231,12 @@
         acc1[block * 2] = total[:, 0:128]
         acc1[block * 2 + 1] = total[:, 128:256]
     spread(acc1, red2, gsend_sem.at[1], grecv_sem.at[1])
-    spread(out_send.at[2], out_recv.at[2], osend_sem.at[2], orecv_sem.at[2])
-    spread(out_send.at[1], out_recv.at[1], osend_sem.at[1], orecv_sem.at[1])
-
-    stores = []
-
-    def unpack(at, target):
-        @pl.loop(0, 8)
+    spread_quarter(2, 2)
+
+    def unpack(at, quarter, target):
+        quarter_arrived(at, quarter)
+
+        @pl.loop(quarter * 2, quarter * 2 + 2)
         def _(pair):
             row = pl.multiple_of(pair * 16, 16)
             firsts, seconds = [], []
@@ -189,25 +245,29 @@
                 firsts.append(both[0:8])
                 seconds.append(both[8:16])
             base = pl.multiple_of(pair * 512, 512)
-            out_stage[at, pl.ds(base, 256), :] = dot(eye_b, jnp.concatenate(firsts, axis=0).astype(BF16), NT).astype(BF16)
-            out_stage[at, pl.ds(base + 256, 256), :] = dot(eye_b, jnp.concatenate(seconds, axis=0).astype(BF16), NT).astype(BF16)
-        copy = pltpu.make_async_copy(out_stage.at[at], target, store_sem.at[at])
-        copy.start()
-        stores.append(copy)
-
-    arrived(out_recv.at[0], orecv_sem.at[0])
-    unpack(0, gi_hbm.at[0])
+            target[pl.ds(base, 256), :] = dot(eye_b, jnp.concatenate(firsts, axis=0).astype(BF16), NT).astype(BF16)
+            target[pl.ds(base + 256, 256), :] = dot(eye_b, jnp.concatenate(seconds, axis=0).astype(BF16), NT).astype(BF16)
+
+    for quarter in range(4):
+        unpack(0, quarter, gi_hbm.at[0])
 
     arrived(red2, grecv_sem.at[1])
     total = red2[0]
     for slot in range(1, 16):
         total = total + red2[slot]
     acc2[...] = total
+    @pl.when(zh == 0)
+    def _():
+        pl.semaphore_wait(entered, 1)
+
     across = pltpu.make_async_remote_copy(
         src_ref=acc2, dst_ref=zbuf, send_sem=gsend_sem.at[2], recv_sem=grecv_sem.at[2],
         device_id={"dp": other_dp}, device_id_type=pl.DeviceIdType.MESH,
     )
     across.start()
+    quarter_drained(2, 0)
+    spread_quarter(2, 3)
+    quarter_drained(2, 1)
     across.wait()
     tot[...] = acc2[...] + zbuf[...]
 
@@ -218,6 +278,10 @@
             device_id={"seq": seq_peer(step)}, device_id_type=pl.DeviceIdType.MESH,
         ).start()
     pltpu.make_async_copy(tot, red3.at[me], grecv_sem.at[3]).start()
+    quarter_drained(2, 2)
+    spread_quarter(1, 0)
+    quarter_drained(2, 3)
+    spread_quarter(1, 1)
     arrived(red3, grecv_sem.at[3])
 
     @pl.loop(1, yc_n)
@@ -227,9 +291,11 @@
             device_id={"dp": zh * yc_n + yc_peer(step)}, device_id_type=pl.DeviceIdType.MESH,
         ).start()
     pltpu.make_async_copy(red3, red4.at[yc], grecv_sem.at[4]).start()
-
-    arrived(out_recv.at[2], orecv_sem.at[2])
-    unpack(2, gk_hbm)
+    spread_quarter(1, 2)
+    spread_quarter(1, 3)
+
+    for quarter in range(4):
+        unpack(2, quarter, gk_hbm)
     arrived(red4, grecv_sem.at[4])
     for slot in range(yc_n):
         for block in range(8):
@@ -237,18 +303,28 @@
             rows = slice((slot % 4) * 64 + block * 8, (slot % 4) * 64 + block * 8 + 8)
             out[rows, 0:128] = red4[slot, block * 2] * scale
             out[rows, 128:256] = red4[slot, block * 2 + 1] * scale
-    arrived(out_recv.at[1], orecv_sem.at[1])
-    unpack(1, gi_hbm.at[1])
-
     for at in range(5):
         drained(send.at[at], recv.at[at], send_sem.at[at])
-    for at in range(3):
-        drained(out_send.at[at], out_recv.at[at], osend_sem.at[at])
+    for quarter in range(4):
+        quarter_drained(0, quarter)
     drained(red1, red1, gsend_sem.at[0])
     drained(red2, red2, gsend_sem.at[1])
     drained(red3, red3, gsend_sem.at[3])
     drained(red4, red4, gsend_sem.at[4])
-    for copy in stores:
+    for quarter in range(4):
+        unpack(1, quarter, gi_hbm.at[1])
+    for quarter in range(4):
+        quarter_drained(1, quarter)
+
+
+def finish(gi, gk, g1, g2, gi_out, gk_out, g1_out, g2_out, sems):
+    copies = [
+        pltpu.make_async_copy(source, target, sems.at[at])
+        for at, (source, target) in enumerate(((gi, gi_out), (gk, gk_out), (g1, g1_out), (g2, g2_out)))
+    ]
+    for copy in copies:
+        copy.start()
+    for copy in copies:
         copy.wait()
 
 
@@ -259,9 +335,14 @@
     scale_one = 1.0 / math.sqrt(batch * factor_two.shape[0] * width)
     scale_two = 1.0 / math.sqrt(batch * factor_one.shape[0] * width)
     anywhere = pl.BlockSpec(memory_space=pl.ANY)
+    far = pl.BlockSpec(memory_space=pltpu.MemorySpace.HBM)
     vmem = pl.BlockSpec(memory_space=pltpu.VMEM)
     square = pltpu.VMEM((2, 2048, 128), F32)
-    return pl.pallas_call(
+    operands = tuple(
+        pltpu.with_memory_space_constraint(value, pltpu.MemorySpace.HBM)
+        for value in (inputs, cotangent, kernel_rows, factor_one, factor_two)
+    )
+    results = pl.pallas_call(
         functools.partial(kernel, seq_n, scale_one, scale_two),
         out_shape=(
             jax.ShapeDtypeStruct(inputs.shape, BF16),
@@ -269,16 +350,17 @@
             jax.ShapeDtypeStruct((256, 256), F32),
             jax.ShapeDtypeStruct((256, 256), F32),
         ),
-        in_specs=[anywhere, anywhere, anywhere, vmem, vmem],
-        out_specs=(anywhere, anywhere, vmem, vmem),
+        in_specs=[far] * 5,
+        out_specs=(vmem, vmem, vmem, vmem),
         scratch_shapes=[
             pltpu.VMEM((5, 4096, 128), BF16),
             pltpu.VMEM((5, 16, 128, 256), BF16),
             pltpu.VMEM((5, 16, 128, 256), BF16),
             pltpu.VMEM((3, 16, 128, 256), BF16),
             pltpu.VMEM((3, 16, 128, 256), BF16),
-            pltpu.VMEM((3, 4096, 128), BF16),
             square, square, square, square, square, square,
+            pltpu.VMEM((256, 256), BF16),
+            pltpu.VMEM((256, 256), BF16),
             pltpu.VMEM((256, 256), BF16),
             pltpu.VMEM((512, 256), F32),
             pltpu.VMEM((8, 64, 256), F32),
@@ -289,19 +371,28 @@
             pltpu.VMEM((8, 128), F32),
             pltpu.VMEM((16, 8, 128), F32),
             pltpu.VMEM((8, 16, 8, 128), F32),
+            pltpu.SemaphoreType.DMA((4,)),
+            pltpu.SemaphoreType.DMA((6,)),
             pltpu.SemaphoreType.DMA((5,)),
             pltpu.SemaphoreType.DMA((5,)),
-            pltpu.SemaphoreType.DMA((5,)),
-            pltpu.SemaphoreType.DMA((3,)),
-            pltpu.SemaphoreType.DMA((3,)),
+            pltpu.SemaphoreType.DMA((3, 4)),
+            pltpu.SemaphoreType.DMA((3, 4)),
             pltpu.SemaphoreType.DMA((5,)),
             pltpu.SemaphoreType.DMA((5,)),
-            pltpu.SemaphoreType.DMA((3,)),
+            pltpu.SemaphoreType.REGULAR,
         ],
         compiler_params=pltpu.CompilerParams(
-            collective_id=0, has_side_effects=True, vmem_limit_bytes=60 * 1024 * 1024
+            collective_id=0, has_side_effects=True, vmem_limit_bytes=42 * 1024 * 1024
         ),
-    )(inputs, cotangent, kernel_rows, factor_one, factor_two)
+    )(*operands)
+    return pl.pallas_call(
+        finish,
+        out_shape=tuple(jax.ShapeDtypeStruct(r.shape, r.dtype) for r in results),
+        in_specs=[anywhere] * 4,
+        out_specs=(far,) * 4,
+        scratch_shapes=[pltpu.SemaphoreType.DMA((4,))],
+        compiler_params=pltpu.CompilerParams(vmem_limit_bytes=4 * 1024 * 1024),
+    )(*results)
 
 
 def solution(mesh):

time: 222 us -> 195 us (0.88); the launches traced: 220 us -> 195 us
  Pallas kernels: 213 us -> 194 us
  local copies, waits for them, and re-layouts: 5.53 us -> 0 us
    pallas_call x1, Pallas kernels: 213 us -> 192 us  [on_device(): pl.pallas_call(functools.partial(kernel, seq_n, scale_one, scale_two), ou...]
    unnamed x10 -> x0, local copies, waits for them, and re-layouts: 5.53 us -> none
where the time goes in v2:
time: 195 us
  Pallas kernels  194 us (99%)
    pallas_call x1, Pallas kernels, on_device(): pl.pallas_call(functools.partial(kernel, seq_n, scale_one, scale_two), ou...  192 us

profile of v2, /device:TPU:2, one launch (start us, length us, event | category | flops | bytes accessed | tf_op | source)
XLA Modules:
  0.0 194.8 jit_solution(6624134808843778739)
XLA Ops:
  0.6 192.3 %shard_map.84 = (bf16[2,4096,128]{2,1,0:T(8,128)(2,1)S(1)}, bf16[4096,128]{1,0:T(8,128)(2,1)S(1)}, f32[256,256]{1,0:T(8,128)S(1)}, f32[256,256]{1,0:T(8,128)S(1)}) custom-call(bf16[2,4096,128]{2,1,0:T(8,128)(2,1)} %x_hbm.1, bf16[2,4096,128]{2,1,0:T(8,128)(2,1)} %y_hbm.1, bf16[4096,128]{1,0:T(8,128)(2,1)} %k_hbm.1, bf16[256,256]{1,0:T(8,128)(2,1)} %f1_hbm.1, ...), custom_call_target="tpu_custom_call" | custom-call | tf_op jit(solution)/shard_map/pallas_call | solution.py:345
  192.9 1.9 shard_map.85

commit v3 on v2

--- a/solution.py
+++ b/solution.py
@@ -34,7 +34,7 @@
     gi_hbm, gk_hbm, g1_out, g2_out,
     stage, send, recv, out_send, out_recv,
     a_buf, g_buf, k_buf, gk_buf, c_buf, v_buf, f1_ref, f2_ref, f2t_ref,
-    gf, red1, acc1, red2, acc2, zbuf, tot, red3, red4,
+    gf, red1, acc1, redx, accx, red2, acc2, zbuf, tot, redz, red3, red4,
     first_sem, load_sem, send_sem, recv_sem, osend_sem, orecv_sem, gsend_sem, grecv_sem, entered,
 ):
     me = lax.axis_index("seq")
@@ -43,6 +43,9 @@
     zh = dp // yc_n
     yc = dp % yc_n
     other_dp = (1 - zh) * yc_n + yc
+
+    x_at = me // 4
+    z_at = me % 4
 
     def seq_peer(step):
         return lax.rem(me + step, seq_n)
@@ -104,7 +107,7 @@
         pltpu.make_async_copy(source.at[me], target.at[me], recv_at).start()
 
     def spread_quarter(at, quarter):
-        rows = pl.ds(quarter * 32, 32)
+        rows = pl.ds(quarter * 16, 16)
 
         @pl.loop(1, seq_n)
         def _(step):
@@ -117,11 +120,11 @@
         pltpu.make_async_copy(out_send.at[at, me, rows], out_recv.at[at, me, rows], orecv_sem.at[at, quarter]).start()
 
     def quarter_arrived(at, quarter):
-        whole = out_recv.at[at, :, pl.ds(quarter * 32, 32)]
+        whole = out_recv.at[at, :, pl.ds(quarter * 16, 16)]
         pltpu.make_async_copy(whole, whole, orecv_sem.at[at, quarter]).wait()
 
     def quarter_drained(at, quarter):
-        rows = pl.ds(quarter * 32, 32)
+        rows = pl.ds(quarter * 16, 16)
         pltpu.make_async_copy(
             out_send.at[at, pl.ds(0, seq_n - 1), rows], out_recv.at[at, pl.ds(0, seq_n - 1), rows], osend_sem.at[at, quarter]
         ).wait()
@@ -205,7 +208,7 @@
     for at in (0, 1, 2):
         arrived(recv.at[at], recv_sem.at[at])
     compute(0, 0, 1)
-    for quarter in range(4):
+    for quarter in range(8):
         spread_quarter(0, quarter)
     for at in (3, 4):
         arrived(recv.at[at], recv_sem.at[at])
@@ -220,8 +223,8 @@
             device_id={"dp": zh * yc_n + peer}, device_id_type=pl.DeviceIdType.MESH,
         ).start()
     pltpu.make_async_copy(gf.at[pl.ds(pl.multiple_of(yc * 64, 64), 64)], red1.at[yc], grecv_sem.at[0]).start()
-    spread_quarter(2, 0)
-    spread_quarter(2, 1)
+    for quarter in range(3):
+        spread_quarter(2, quarter)
     arrived(red1, grecv_sem.at[0])
     for block in range(8):
         rows = slice(block * 8, block * 8 + 8)
@@ -230,13 +233,33 @@
             total = total + red1[slot, rows, :]
         acc1[block * 2] = total[:, 0:128]
         acc1[block * 2 + 1] = total[:, 128:256]
-    spread(acc1, red2, gsend_sem.at[1], grecv_sem.at[1])
-    spread_quarter(2, 2)
+    @pl.loop(1, 4)
+    def _(step):
+        peer = lax.rem(x_at + step, 4)
+        pltpu.make_async_remote_copy(
+            src_ref=acc1.at[pl.ds(peer * 4, 4)], dst_ref=redx.at[x_at], send_sem=gsend_sem.at[1], recv_sem=grecv_sem.at[1],
+            device_id={"seq": peer * 4 + z_at}, device_id_type=pl.DeviceIdType.MESH,
+        ).start()
+    pltpu.make_async_copy(acc1.at[pl.ds(x_at * 4, 4)], redx.at[x_at], grecv_sem.at[1]).start()
+    spread_quarter(2, 3)
+    spread_quarter(2, 4)
+    arrived(redx, grecv_sem.at[1])
+    accx[...] = redx[0] + redx[1] + redx[2] + redx[3]
+
+    @pl.loop(1, 4)
+    def _(step):
+        peer = lax.rem(z_at + step, 4)
+        pltpu.make_async_remote_copy(
+            src_ref=accx.at[peer], dst_ref=red2.at[z_at], send_sem=gsend_sem.at[5], recv_sem=grecv_sem.at[5],
+            device_id={"seq": x_at * 4 + peer}, device_id_type=pl.DeviceIdType.MESH,
+        ).start()
+    pltpu.make_async_copy(accx.at[z_at], red2.at[z_at], grecv_sem.at[5]).start()
+    spread_quarter(2, 5)
 
     def unpack(at, quarter, target):
         quarter_arrived(at, quarter)
 
-        @pl.loop(quarter * 2, quarter * 2 + 2)
+        @pl.loop(quarter, quarter + 1)
         def _(pair):
             row = pl.multiple_of(pair * 16, 16)
             firsts, seconds = [], []
@@ -248,12 +271,12 @@
             target[pl.ds(base, 256), :] = dot(eye_b, jnp.concatenate(firsts, axis=0).astype(BF16), NT).astype(BF16)
             target[pl.ds(base + 256, 256), :] = dot(eye_b, jnp.concatenate(seconds, axis=0).astype(BF16), NT).astype(BF16)
 
-    for quarter in range(4):
+    for quarter in range(8):
         unpack(0, quarter, gi_hbm.at[0])
 
-    arrived(red2, grecv_sem.at[1])
+    arrived(red2, grecv_sem.at[5])
     total = red2[0]
-    for slot in range(1, 16):
+    for slot in range(1, 4):
         total = total + red2[slot]
     acc2[...] = total
     @pl.when(zh == 0)
@@ -265,23 +288,32 @@
         device_id={"dp": other_dp}, device_id_type=pl.DeviceIdType.MESH,
     )
     across.start()
-    quarter_drained(2, 0)
-    spread_quarter(2, 3)
-    quarter_drained(2, 1)
+    spread_quarter(2, 6)
+    spread_quarter(2, 7)
     across.wait()
     tot[...] = acc2[...] + zbuf[...]
 
-    @pl.loop(1, seq_n)
-    def _(step):
-        pltpu.make_async_remote_copy(
-            src_ref=tot, dst_ref=red3.at[me], send_sem=gsend_sem.at[3], recv_sem=grecv_sem.at[3],
-            device_id={"seq": seq_peer(step)}, device_id_type=pl.DeviceIdType.MESH,
-        ).start()
-    pltpu.make_async_copy(tot, red3.at[me], grecv_sem.at[3]).start()
-    quarter_drained(2, 2)
+    @pl.loop(1, 4)
+    def _(step):
+        peer = lax.rem(z_at + step, 4)
+        pltpu.make_async_remote_copy(
+            src_ref=tot, dst_ref=redz.at[z_at], send_sem=gsend_sem.at[6], recv_sem=grecv_sem.at[6],
+            device_id={"seq": x_at * 4 + peer}, device_id_type=pl.DeviceIdType.MESH,
+        ).start()
+    pltpu.make_async_copy(tot, redz.at[z_at], grecv_sem.at[6]).start()
     spread_quarter(1, 0)
-    quarter_drained(2, 3)
     spread_quarter(1, 1)
+    arrived(redz, grecv_sem.at[6])
+
+    @pl.loop(1, 4)
+    def _(step):
+        peer = lax.rem(x_at + step, 4)
+        pltpu.make_async_remote_copy(
+            src_ref=redz, dst_ref=red3.at[x_at], send_sem=gsend_sem.at[3], recv_sem=grecv_sem.at[3],
+            device_id={"seq": peer * 4 + z_at}, device_id_type=pl.DeviceIdType.MESH,
+        ).start()
+    pltpu.make_async_copy(redz, red3.at[x_at], grecv_sem.at[3]).start()
+    spread_quarter(1, 2)
     arrived(red3, grecv_sem.at[3])
 
     @pl.loop(1, yc_n)
@@ -291,29 +323,32 @@
             device_id={"dp": zh * yc_n + yc_peer(step)}, device_id_type=pl.DeviceIdType.MESH,
         ).start()
     pltpu.make_async_copy(red3, red4.at[yc], grecv_sem.at[4]).start()
-    spread_quarter(1, 2)
-    spread_quarter(1, 3)
-
-    for quarter in range(4):
+    for quarter in range(3, 8):
+        spread_quarter(1, quarter)
+
+    for quarter in range(8):
         unpack(2, quarter, gk_hbm)
     arrived(red4, grecv_sem.at[4])
     for slot in range(yc_n):
         for block in range(8):
             out, scale = (g1_out, scale_one) if slot < 4 else (g2_out, scale_two)
             rows = slice((slot % 4) * 64 + block * 8, (slot % 4) * 64 + block * 8 + 8)
-            out[rows, 0:128] = red4[slot, block * 2] * scale
-            out[rows, 128:256] = red4[slot, block * 2 + 1] * scale
+            out[rows, 0:128] = red4[slot, (block * 2) // 4, (block * 2) % 4] * scale
+            out[rows, 128:256] = red4[slot, (block * 2 + 1) // 4, (block * 2 + 1) % 4] * scale
     for at in range(5):
         drained(send.at[at], recv.at[at], send_sem.at[at])
-    for quarter in range(4):
+    for quarter in range(8):
         quarter_drained(0, quarter)
+        quarter_drained(2, quarter)
     drained(red1, red1, gsend_sem.at[0])
-    drained(red2, red2, gsend_sem.at[1])
+    drained(redx, redx, gsend_sem.at[1])
+    drained(red2, red2, gsend_sem.at[5])
+    drained(redz, redz, gsend_sem.at[6])
     drained(red3, red3, gsend_sem.at[3])
     drained(red4, red4, gsend_sem.at[4])
-    for quarter in range(4):
+    for quarter in range(8):
         unpack(1, quarter, gi_hbm.at[1])
-    for quarter in range(4):
+    for quarter in range(8):
         quarter_drained(1, quarter)
 
 
@@ -365,20 +400,23 @@
             pltpu.VMEM((512, 256), F32),
             pltpu.VMEM((8, 64, 256), F32),
             pltpu.VMEM((16, 8, 128), F32),
-            pltpu.VMEM((16, 8, 128), F32),
+            pltpu.VMEM((4, 4, 8, 128), F32),
+            pltpu.VMEM((4, 8, 128), F32),
+            pltpu.VMEM((4, 8, 128), F32),
             pltpu.VMEM((8, 128), F32),
             pltpu.VMEM((8, 128), F32),
             pltpu.VMEM((8, 128), F32),
-            pltpu.VMEM((16, 8, 128), F32),
-            pltpu.VMEM((8, 16, 8, 128), F32),
+            pltpu.VMEM((4, 8, 128), F32),
+            pltpu.VMEM((4, 4, 8, 128), F32),
+            pltpu.VMEM((8, 4, 4, 8, 128), F32),
             pltpu.SemaphoreType.DMA((4,)),
             pltpu.SemaphoreType.DMA((6,)),
             pltpu.SemaphoreType.DMA((5,)),
             pltpu.SemaphoreType.DMA((5,)),
-            pltpu.SemaphoreType.DMA((3, 4)),
-            pltpu.SemaphoreType.DMA((3, 4)),
-            pltpu.SemaphoreType.DMA((5,)),
-            pltpu.SemaphoreType.DMA((5,)),
+            pltpu.SemaphoreType.DMA((3, 8)),
+            pltpu.SemaphoreType.DMA((3, 8)),
+            pltpu.SemaphoreType.DMA((7,)),
+            pltpu.SemaphoreType.DMA((7,)),
             pltpu.SemaphoreType.REGULAR,
         ],
         compiler_params=pltpu.CompilerParams(

time: 195 us -> 195 us (level)
  no operation moved by 1% of the time
where the time goes in v3:
time: 195 us; the launch traced here: 194 us
  Pallas kernels  193 us (99%)
    pallas_call x1, Pallas kernels, on_device(): pl.pallas_call(functools.partial(kernel, seq_n, scale_one, scale_two), ou...  191 us

profile of v3, /device:TPU:2, one launch (start us, length us, event | category | flops | bytes accessed | tf_op | source)
XLA Modules:
  0.0 193.7 jit_solution(17827906188674990243)
XLA Ops:
  0.6 191.2 %shard_map.84 = (bf16[2,4096,128]{2,1,0:T(8,128)(2,1)S(1)}, bf16[4096,128]{1,0:T(8,128)(2,1)S(1)}, f32[256,256]{1,0:T(8,128)S(1)}, f32[256,256]{1,0:T(8,128)S(1)}) custom-call(bf16[2,4096,128]{2,1,0:T(8,128)(2,1)} %x_hbm.1, bf16[2,4096,128]{2,1,0:T(8,128)(2,1)} %y_hbm.1, bf16[4096,128]{1,0:T(8,128)(2,1)} %k_hbm.1, bf16[256,256]{1,0:T(8,128)(2,1)} %f1_hbm.1, ...), custom_call_target="tpu_custom_call" | custom-call | tf_op jit(solution)/shard_map/pallas_call | solution.py:380
  191.9 1.9 shard_map.85
